TPU v7x, 512 devices: a whole 4x4x16 slice. The times are simulated.
512 devices in a mesh: ctx: 16 (over y, x), head: 32 (over z, core).
Axes of the slice: x: 4, y: 4, z: 16, core: 2. Of those that a mesh axis runs over, the one named last changes fastest.
Arguments:
- doc_lengths: int32 [4], replicated, may hold values from 1 to 6144, 8192 in all
- lin_q: bfloat16 [8192, 8192], P('ctx', 'head'), may hold values from -6 to 6
- lin_k: bfloat16 [8192, 8192], P('ctx', 'head'), may hold values from -6 to 6
- lin_v: bfloat16 [8192, 8192], P('ctx', 'head'), may hold values from -40 to 40
- log_decay: float32 [64, 8192], P('head', 'ctx'), may hold values from -1 to 0
- lin_gain: float32 [8192], P('head'), may hold values from 0.5 to 1.5
- soft_q: bfloat16 [8192, 8192], P('ctx', 'head'), may hold values from -48 to 48
- soft_k: bfloat16 [8192, 1024], P('ctx', 'head'), may hold values from -6 to 6
- soft_v: bfloat16 [8192, 1024], P('ctx', 'head'), may hold values from -6 to 6
Outputs:
- lin_out: bfloat16 [8192, 8192], P('ctx', 'head')
- soft_out: bfloat16 [8192, 8192], P('ctx', 'head')
Inputs may be any that keep to these rules, and one draw needn't show every extreme that they name: `doc_lengths`: the 4 lengths sum to 8192 and the largest is exactly 6144.
All inputs are finite; a program needn't handle non-finite values.
Results may differ from a plain program's by a relative error of at most 0.015.
Values may be sent and summed in bfloat16 or wider, within the bound.
A program may use at most 64 MiB of HBM per device.

v0:
```python
import jax
import jax.numpy as jnp
from jax import lax
from jax.sharding import PartitionSpec as P

KVH = 8
DH = 128
BLK = 256


def prefix(value, axis, join, neutral):
    place = lax.axis_index(axis)
    gathered = jax.tree.map(
        lambda a, kind: lax.all_gather(a.astype(kind), axis), value, (jnp.bfloat16, jnp.bfloat16)
    )
    state = jax.tree.map(lambda a, e: jnp.zeros_like(a) + jnp.asarray(e, a.dtype), value, neutral)

    def one(turn, state):
        return join(
            state,
            jax.tree.map(
                lambda a, own: lax.dynamic_index_in_dim(a, turn, 0, False).astype(own.dtype),
                gathered,
                value,
            ),
        )

    return lax.fori_loop(0, place, one, state)


def swapped(value, axis, stride):
    return lax.ppermute(value, axis, [(i, i ^ 1 << stride) for i in range(lax.axis_size(axis))])


def doc_index(doc_lengths, positions):
    bounds = jnp.cumsum(doc_lengths)
    counted = jnp.sum((bounds[None, :] <= positions[:, None]).astype(jnp.int32), axis=1)
    return jnp.where(positions < 0, -1, counted)


def lightning_parts(queries, keys_block, values_block, decay_block, segs_block, seg_before):
    running = jnp.cumsum(decay_block, axis=1)
    block_len = segs_block.shape[0]
    rows_iota = lax.broadcasted_iota(jnp.int32, (block_len, block_len), 0)
    cols_iota = lax.broadcasted_iota(jnp.int32, (block_len, block_len), 1)
    allowed = (rows_iota >= cols_iota) & (segs_block[:, None] == segs_block[None, :])
    spread = jnp.where(allowed[None], running[:, :, None] - running[:, None, :], 0.0)
    decays = jnp.where(allowed[None], jnp.exp(spread), 0.0)
    scores = (
        jnp.einsum("ihd,jhd->hij", queries, keys_block, preferred_element_type=jnp.float32) * decays
    )
    scores = scores.astype(jnp.bfloat16)
    inside = jnp.einsum("hij,jhd->ihd", scores, values_block, preferred_element_type=jnp.float32)
    carried = (segs_block == seg_before).astype(jnp.float32)
    entering = jnp.exp(running) * carried[None, :]
    closing = running[:, -1:]
    tail_mask = (segs_block == segs_block[-1]).astype(jnp.float32)
    weights = jnp.exp(closing - running) * tail_mask[None, :]
    weighted = (keys_block * weights.T[:, :, None]).astype(jnp.bfloat16)
    update = jnp.einsum("jhd,jhe->hde", weighted, values_block, preferred_element_type=jnp.float32)
    kept_flag = (segs_block[-1] == seg_before).astype(jnp.float32)
    decay_factor = kept_flag * jnp.exp(closing[:, 0])
    return (inside, entering, update, decay_factor)


def local(doc_lengths, lin_q, lin_k, lin_v, log_decay, lin_gain, soft_q, soft_k, soft_v):
    tok_count = lin_q.shape[0]
    heads_here = lin_gain.shape[0] // DH
    ctx_place = lax.axis_index("ctx")
    positions = ctx_place * tok_count + jnp.arange(tok_count, dtype=jnp.int32)
    doc_ids = doc_index(doc_lengths, positions)
    seg_previous = doc_index(doc_lengths, positions[:1] - 1)[0]
    query_rows = lin_q.reshape(tok_count, heads_here, DH)
    key_rows = lin_k.reshape(tok_count, heads_here, DH)
    value_rows = lin_v.reshape(tok_count, heads_here, DH)
    blocks = tok_count // BLK
    pieces_list = []
    local_state = jnp.zeros((heads_here, DH, DH), jnp.float32)
    through = jnp.ones((heads_here,), jnp.float32)
    for number in range(blocks):
        first_row = number * BLK
        last_row = first_row + BLK
        seg_before = seg_previous if number == 0 else doc_ids[first_row - 1]
        parts_now = lightning_parts(
            query_rows[first_row:last_row],
            key_rows[first_row:last_row],
            value_rows[first_row:last_row],
            log_decay[:, first_row:last_row],
            doc_ids[first_row:last_row],
            seg_before,
        )
        pieces_list.append(parts_now)
        local_state = parts_now[3][:, None, None] * local_state + parts_now[2]
        through = through * parts_now[3]
    empty_state = jnp.zeros((heads_here, DH, DH), jnp.float32)

    def combine(earlier, later):
        return (earlier[0] * later[0], later[0][:, None, None] * earlier[1] + later[1])

    incoming = prefix(
        (through, local_state), "ctx", combine, (jnp.ones((heads_here,), jnp.float32), empty_state)
    )
    carry_state = incoming[1]
    outputs = []
    for number in range(blocks):
        first_row = number * BLK
        inside, entering, update, decay_factor = pieces_list[number]
        across = jnp.einsum(
            "ihd,hde->ihe",
            query_rows[first_row : first_row + BLK],
            carry_state.astype(jnp.bfloat16),
            preferred_element_type=jnp.float32,
        )
        outputs.append(inside + across * entering.T[:, :, None])
        carry_state = decay_factor[:, None, None] * carry_state + update
    raw_out = jnp.concatenate(outputs, axis=0)
    norm_scale = lax.rsqrt(jnp.mean(raw_out * raw_out, axis=2, keepdims=True) + 1e-06)
    lin_out = (
        (raw_out * norm_scale * lin_gain.reshape(1, heads_here, DH))
        .reshape(tok_count, heads_here * DH)
        .astype(jnp.bfloat16)
    )
    head_place = lax.axis_index("head")
    group_width = lax.axis_size("head") // KVH
    bit_count = group_width.bit_length() - 1
    own_keys, own_values = (soft_k, soft_v)
    for bit in range(bit_count):
        far_keys, far_values = swapped((own_keys, own_values), "head", bit)
        upper = head_place // (1 << bit) % 2 == 1
        own_keys = jnp.where(
            upper,
            jnp.concatenate([far_keys, own_keys], axis=1),
            jnp.concatenate([own_keys, far_keys], axis=1),
        )
        own_values = jnp.where(
            upper,
            jnp.concatenate([far_values, own_values], axis=1),
            jnp.concatenate([own_values, far_values], axis=1),
        )
    soft_rows = soft_q.reshape(tok_count, heads_here, DH)

    def attend(softmax_state, key_piece, value_piece, key_start):
        row_top, row_total, accum_rows = softmax_state
        key_pos = key_start + jnp.arange(key_piece.shape[0], dtype=jnp.int32)
        key_doc = doc_index(doc_lengths, key_pos)
        scores = jnp.einsum(
            "ihd,jd->hij", soft_rows, key_piece, preferred_element_type=jnp.float32
        ) * DH ** (-0.5)
        allowed = (key_pos[None, :] <= positions[:, None]) & (key_doc[None, :] == doc_ids[:, None])
        masked = jnp.where(allowed[None], scores, -1e30)
        new_top = jnp.maximum(row_top, jnp.max(masked, axis=2))
        exp_terms = jnp.where(allowed[None], jnp.exp(scores - new_top[:, :, None]), 0.0)
        rescale = jnp.exp(row_top - new_top)
        new_total = rescale * row_total + jnp.sum(exp_terms, axis=2)
        new_accum = rescale[:, :, None] * accum_rows + jnp.einsum(
            "hij,jd->hid",
            exp_terms.astype(jnp.bfloat16),
            value_piece,
            preferred_element_type=jnp.float32,
        )
        return (new_top, new_total, new_accum)

    def visit(softmax_state, key_piece, value_piece, key_start):
        return attend(softmax_state, key_piece, value_piece, key_start)

    start_state = (
        jnp.full((heads_here, tok_count), -1e30, jnp.float32),
        jnp.zeros((heads_here, tok_count), jnp.float32),
        jnp.zeros((heads_here, tok_count, DH), jnp.float32),
    )
    key_piece = lax.all_gather(own_keys, "ctx", axis=0, tiled=True)
    value_piece = lax.all_gather(own_values, "ctx", axis=0, tiled=True)
    row_count = key_piece.shape[0]

    def inner_visit(state_in, scan_items):
        offset, key_part, value_part = scan_items
        return (visit(state_in, key_part, value_part, offset), None)

    offsets = jnp.arange(row_count // 512, dtype=jnp.int32) * 512
    result, _ = lax.scan(
        inner_visit,
        start_state,
        (
            offsets,
            key_piece.reshape(row_count // 512, 512, DH),
            value_piece.reshape(row_count // 512, 512, DH),
        ),
    )
    final_top, final_total, final_accum = result
    soft_out = (
        (final_accum / final_total[:, :, None])
        .transpose(1, 0, 2)
        .reshape(tok_count, heads_here * DH)
        .astype(jnp.bfloat16)
    )
    return (lin_out, soft_out)


def solution(mesh):
    placed = (
        P(),
        P("ctx", "head"),
        P("ctx", "head"),
        P("ctx", "head"),
        P("head", "ctx"),
        P("head"),
        P("ctx", "head"),
        P("ctx", "head"),
        P("ctx", "head"),
    )
    return jax.shard_map(
        local,
        mesh=mesh,
        in_specs=placed,
        out_specs=(P("ctx", "head"), P("ctx", "head")),
        check_vma=False,
    )
```

profile of v0, /device:TPU:1, one launch (start us, length us, event | category | flops | bytes accessed | tf_op | source)
XLA Modules:
  0.0 323.4 jit_solution(9549522584730469660)
XLA Ops:
  7.8 0.8 reduce-window.19
  8.7 0.7 fusion.69
  12.6 1.3 compare_convert_fusion.1
  14.6 0.7 fusion.67
  17.8 1.0 fusion.65
  18.9 1.0 fusion.66
  20.6 0.8 fusion.33
  21.5 8.8 %collective-permute-start = (bf16[512,32]{0,1:T(8,128)(2,1)S(1)}, bf16[512,32]{0,1:T(8,128)(2,1)S(1)}, u32[]{:S(2)}, u32[]{:S(2)}) collective-permute-start(bf16[512,32]{0,1:T(8,128)(2,1)S(1)} %copy-done.2), channel_id=1, source_target_pairs={{0,1},{1,0},{2,3},{3,2},{4,5},{5,4},{6,7},{7,6},{8,9},{9,8},{10,11... | collective-permute-start | bytes 98312 | tf_op jit(solution)/shard_map/ppermute | solution.py:32
  30.3 0.8 collective-permute-done
  31.1 1.9 collective-permute-start.1
  33.1 3.1 collective-permute-done.1
  36.1 0.7 maximum_select_fusion
  36.9 3.4 %collective-permute-start.2 = (bf16[512,32]{0,1:T(8,128)(2,1)S(1)}, bf16[512,32]{0,1:T(8,128)(2,1)S(1)}, u32[]{:S(2)}, u32[]{:S(2)}) collective-permute-start(bf16[512,32]{0,1:T(8,128)(2,1)S(1)} %copy-done.3), channel_id=1, source_target_pairs={{0,1},{1,0},{2,3},{3,2},{4,5},{5,4},{6,7},{7,6},{8,9},{9,8},{10,11... | collective-permute-start | bytes 98312 | tf_op jit(solution)/shard_map/ppermute | solution.py:32
  40.3 0.8 collective-permute-done.2
  41.2 1.9 collective-permute-start.3
  43.1 3.1 collective-permute-done.3
  46.2 0.7 maximum_select_fusion.1
  46.9 1.3 dynamic-slice
  49.1 28.6 %all-reduce = bf16[32]{0:T(256)(128)(2,1)S(1)} all-reduce(bf16[32]{0:T(256)(128)(2,1)S(1)} %dynamic-update-slice), channel_id=2, replica_groups=mesh['ctx'=16,'head'=32] {'ctx'}, use_global_device_ids=true, to_apply=%add | all-reduce | flops 32 | bytes 128
  78.7 4.9 %all-gather.10.cloned.1.call-done = bf16[32,128,128]{2,1,0:T(8,128)(2,1)} async-done(((bf16[2,128,128]{2,1,0:T(8,128)(2,1)}), bf16[32,128,128]{2,1,0:T(8,128)(2,1)}) %all-gather.10.cloned.1.call-update) | async-done | bytes 1048592 | tf_op jit(solution)/shard_map/all_gather | solution.py:14
  86.3 0.8 fusion.35
  87.0 62.9 %all-gather.6.cloned.1.call-done = bf16[8192,128]{0,1:T(8,128)(2,1)} async-done(((bf16[512,128]{0,1:T(8,128)(2,1)}), bf16[8192,128]{0,1:T(8,128)(2,1)}) %all-gather.6.cloned.1.call-update) | async-done | bytes 2097168 | tf_op jit(solution)/shard_map/all_gather | solution.py:171
  150.0 4.1 %copy.122 = bf16[8192,128]{1,0:T(8,128)(2,1)} copy(bf16[8192,128]{0,1:T(8,128)(2,1)} %all-gather.6.cloned.1.call-done) | data formatting | bytes 4194304 | tf_op jit(solution)/shard_map/all_gather | solution.py:171
  154.1 61.4 %all-gather.8.cloned.1.call-done = bf16[8192,128]{0,1:T(8,128)(2,1)} async-done(((bf16[512,128]{0,1:T(8,128)(2,1)}), bf16[8192,128]{0,1:T(8,128)(2,1)}) %all-gather.8.cloned.1.call-update) | async-done | bytes 2097168 | tf_op jit(solution)/shard_map/all_gather | solution.py:172
  215.5 4.1 %copy.124 = bf16[8192,128]{1,0:T(8,128)(2,1)} copy(bf16[8192,128]{0,1:T(8,128)(2,1)} %all-gather.8.cloned.1.call-done) | data formatting | bytes 4194304 | tf_op jit(solution)/shard_map/all_gather | solution.py:172
  219.5 96.5 %while.30 = (s32[]{:T(128)}, f32[2,512]{1,0:T(2,128)S(1)}, f32[2,512]{1,0:T(2,128)S(1)}, f32[2,512,128]{2,1,0:T(8,128)S(1)}, s32[16]{0:T(128)S(1)}, /*index=5*/s...) while((s32[]{:T(128)}, f32[2,512]{1,0:T(2,128)S(1)}, ...), condition=%wide.region_15.16_spmd.clone, body=%wide.region_11.15_spmd.clone.sunk | while | flops 275395584 | bytes 9000113 | solution.py:180
  220.9 0.6 compare_select_fusion.3
  221.8 1.5 fusion.92
  223.8 1.7 convolution_add_fusion.3
  226.9 0.6 compare_select_fusion.3
  227.8 1.5 fusion.92
  229.8 1.7 convolution_add_fusion.3
  232.9 0.6 compare_select_fusion.3
  233.9 1.5 fusion.92
  235.9 1.7 convolution_add_fusion.3
  238.9 0.6 compare_select_fusion.3
  239.9 1.5 fusion.92
  241.9 1.7 convolution_add_fusion.3
  245.9 1.5 fusion.92
  247.9 1.7 convolution_add_fusion.3
  252.0 1.5 fusion.92
  253.9 1.7 convolution_add_fusion.3
  258.0 1.5 fusion.92
  260.0 1.7 convolution_add_fusion.3
  264.0 1.5 fusion.92
  266.0 1.7 convolution_add_fusion.3
  270.0 1.5 fusion.92
  272.0 1.7 convolution_add_fusion.3
  276.1 1.5 fusion.92
  278.1 1.7 convolution_add_fusion.3
  282.1 1.5 fusion.92
  284.1 1.7 convolution_add_fusion.3
  288.1 1.5 fusion.92
  290.1 1.7 convolution_add_fusion.3
  294.2 1.5 fusion.92
  296.2 1.7 convolution_add_fusion.3
  299.2 0.6 compare_select_fusion.3
  300.2 1.5 fusion.92
  302.2 1.7 convolution_add_fusion.3
  306.2 1.5 fusion.92
  308.2 1.7 convolution_add_fusion.3
  312.2 1.5 fusion.92
  314.2 1.7 convolution_add_fusion.3
  316.0 0.9 copy_bitcast_fusion
  (215 shorter events, 49.4 us)
Async XLA Ops:
  7.2 14.3 %copy-start.2 = (bf16[512,32]{0,1:T(8,128)(2,1)S(1)}, bf16[512,32]{0,1:T(8,128)(2,1)}, u32[]{:S(2)}) copy-start(bf16[512,32]{0,1:T(8,128)(2,1)} %param.20) | copy-start | bytes 98308
  7.2 29.7 %copy-start.3 = (bf16[512,32]{0,1:T(8,128)(2,1)S(1)}, bf16[512,32]{0,1:T(8,128)(2,1)}, u32[]{:S(2)}) copy-start(bf16[512,32]{0,1:T(8,128)(2,1)} %param.21) | copy-start | bytes 98308
  7.2 76.5 %all-gather.10.cloned.1.call-start = ((), (), s32[]{:S(2)}) async-start(), calls=%async_computation.2 | async-start | bytes 1114112 | tf_op jit(solution)/shard_map/all_gather | solution.py:14
  17.8 59.9 %copy-start = (bf16[512,256]{1,0:T(8,128)(2,1)S(1)}, bf16[512,256]{1,0:T(8,128)(2,1)}, u32[]{:S(2)}) copy-start(bf16[512,256]{1,0:T(8,128)(2,1)} %param.19) | copy-start | bytes 786436
  19.9 58.1 %copy-start.5 = (s32[4]{0:T(128)S(1)}, s32[4]{0:T(128)}, u32[]{:S(2)}) copy-start(s32[4]{0:T(128)} %param.13) | copy-start | bytes 52
  19.9 58.4 %copy-start.1 = (bf16[512,256]{1,0:T(8,128)(2,1)S(1)}, bf16[512,256]{1,0:T(8,128)(2,1)}, u32[]{:S(2)}) copy-start(bf16[512,256]{1,0:T(8,128)(2,1)} %param.14) | copy-start | bytes 786436
  21.4 128.6 %all-gather.6.cloned.1.call-start = ((), (), s32[]{:S(2)}) async-start(), calls=%async_computation | async-start | bytes 2228224 | tf_op jit(solution)/shard_map/all_gather | solution.py:171
  21.5 9.6 %collective-permute-start = (bf16[512,32]{0,1:T(8,128)(2,1)S(1)}, bf16[512,32]{0,1:T(8,128)(2,1)S(1)}, u32[]{:S(2)}, u32[]{:S(2)}) collective-permute-start(bf16[512,32]{0,1:T(8,128)(2,1)S(1)} %copy-done.2), channel_id=1, source_target_pairs={{0,1},{1,0},{2,3},{3,2},{4,5},{5,4},{6,7},{7,6},{8,9},{9,8},{10,11... | collective-permute-start | bytes 98312 | tf_op jit(solution)/shard_map/ppermute | solution.py:32
  31.1 5.0 %collective-permute-start.1 = (bf16[512,64]{0,1:T(8,128)(2,1)S(1)}, bf16[512,64]{0,1:T(8,128)(2,1)S(1)}, u32[]{:S(2)}, u32[]{:S(2)}) collective-permute-start(bf16[512,64]{0,1:T(8,128)(2,1)S(1)} %maximum_select_fusion.2), channel_id=1, source_target_pairs={{0,2},{1,3},{2,0},{3,1},{4,6},{5,7},{6,4},{7,5},{8,10},{9,11},{10,... | collective-permute-start | bytes 196616 | tf_op jit(solution)/shard_map/ppermute | solution.py:32
  36.8 178.6 %all-gather.8.cloned.1.call-start = ((), (), s32[]{:S(2)}) async-start(), calls=%async_computation.1 | async-start | bytes 2228224 | tf_op jit(solution)/shard_map/all_gather | solution.py:172
  36.9 4.3 %collective-permute-start.2 = (bf16[512,32]{0,1:T(8,128)(2,1)S(1)}, bf16[512,32]{0,1:T(8,128)(2,1)S(1)}, u32[]{:S(2)}, u32[]{:S(2)}) collective-permute-start(bf16[512,32]{0,1:T(8,128)(2,1)S(1)} %copy-done.3), channel_id=1, source_target_pairs={{0,1},{1,0},{2,3},{3,2},{4,5},{5,4},{6,7},{7,6},{8,9},{9,8},{10,11... | collective-permute-start | bytes 98312 | tf_op jit(solution)/shard_map/ppermute | solution.py:32
  41.2 5.0 %collective-permute-start.3 = (bf16[512,64]{0,1:T(8,128)(2,1)S(1)}, bf16[512,64]{0,1:T(8,128)(2,1)S(1)}, u32[]{:S(2)}, u32[]{:S(2)}) collective-permute-start(bf16[512,64]{0,1:T(8,128)(2,1)S(1)} %maximum_select_fusion.3), channel_id=1, source_target_pairs={{0,2},{1,3},{2,0},{3,1},{4,6},{5,7},{6,4},{7,5},{8,10},{9,11},{10,... | collective-permute-start | bytes 196616 | tf_op jit(solution)/shard_map/ppermute | solution.py:32
  84.7 1.6 copy-start.4
Sparse Core Ops, SparseCore 0:
  21.5 62.0 all-gather.9
  87.2 62.7 all-gather.5
  153.0 62.4 all-gather.7
where the time goes:
time: 326 us; the launch traced here: 323 us
  waiting for transfers between devices  137 us (42%)
  matrix products  53.5 us (16%)
  other arithmetic  43.1 us (13%)
  blocking collectives  28.6 us (9%)
  local copies, waits for them, and re-layouts  25.8 us (8%)
  between operations  18.1 us (6%)
  starting transfers between devices  16.2 us (5%)
    all_gather x1, waiting for transfers between devices, local(): key_piece = lax.all_gather(own_keys, 'ctx', axis=0, tiled=True)  62.9 us
    all_gather x1, waiting for transfers between devices, local(): value_piece = lax.all_gather(own_values, 'ctx', axis=0, tiled=True)  61.4 us
    unnamed x1, blocking collectives  28.6 us
    dot_general x16, matrix products, attend(): jnp.einsum('hij,jd->hid', exp_terms.astype(jnp.bfloat16), value_piece, pr...  27.7 us
    dot_general x16, matrix products, attend(): jnp.einsum('ihd,jd->hij', soft_rows, key_piece, preferred_element_type=jn...  23.3 us
    ppermute x4, starting transfers between devices, swapped(): lax.ppermute(value, axis, [(i, i ^ 1 << stride) for i in range(lax.axis_s...  16 us
    select_n x17, other arithmetic, doc_index(): return jnp.where(positions < 0, -1, counted)  10.4 us
    add x17, other arithmetic, local(): positions = ctx_place * tok_count + jnp.arange(tok_count, dtype=jnp.int32)  10.4 us
  transfers between devices with their start and end apart: 7, of which 7 were waited for; matrix products, arithmetic and copies ran while one was open for 3% of the time, Pallas kernels for 0%

commit v1 on v0

--- a/solution.py
+++ b/solution.py
@@ -1,3 +1,4 @@
+import functools
 import jax
 import jax.numpy as jnp
 from jax import lax
@@ -6,6 +7,24 @@
 KVH = 8
 DH = 128
 BLK = 256
+
+
+def set_balance(slab_in, peer_axis):
+    kept_rows = [slab_in]
+    workers = lax.axis_size(peer_axis)
+    for u in tuple(range(workers - 1)):
+        kept_rows.append(
+            lax.ppermute(
+                kept_rows[-1],
+                axis_name=peer_axis,
+                perm=[(dev, (dev + 1) % workers) for dev in range(workers)],
+            )
+        )
+    local_now = jnp.concatenate(kept_rows[::-1], 0)
+    return jnp.roll(local_now, (lax.axis_index(peer_axis) + 1) * slab_in.shape[0], 0)
+
+
+follow_tracks_in = functools.partial(set_balance, peer_axis="ctx")
 
 
 def prefix(value, axis, join, neutral):
@@ -169,7 +188,7 @@
         jnp.zeros((heads_here, tok_count, DH), jnp.float32),
     )
     key_piece = lax.all_gather(own_keys, "ctx", axis=0, tiled=True)
-    value_piece = lax.all_gather(own_values, "ctx", axis=0, tiled=True)
+    value_piece = follow_tracks_in(own_values)
     row_count = key_piece.shape[0]
 
     def inner_visit(state_in, scan_items):

time: 326 us -> 388 us (1.19)
  starting transfers between devices: 16.2 us -> 55.1 us
  local copies, waits for them, and re-layouts: 25.8 us -> 34.9 us
  blocking collectives: 28.6 us -> 34.2 us
  other arithmetic: 43.1 us -> 48.5 us
  matrix products: 53.5 us -> 58.6 us
    ppermute x0 -> x15, waiting for transfers between devices: none -> 77.7 us  [set_balance(): lax.ppermute(kept_rows[-1], axis_name=peer_axis, perm=[(dev, (dev + 1) %...]
    all_gather x1 -> x0, waiting for transfers between devices: 61.4 us -> none  [local(): value_piece = lax.all_gather(own_values, 'ctx', axis=0, tiled=True)]
    ppermute x0 -> x15, starting transfers between devices: none -> 28.7 us  [set_balance(): lax.ppermute(kept_rows[-1], axis_name=peer_axis, perm=[(dev, (dev + 1) %...]
    ppermute x4, starting transfers between devices: 16 us -> 26.4 us  [swapped(): lax.ppermute(value, axis, [(i, i ^ 1 << stride) for i in range(lax.axis_s...]
    unnamed x26 -> x59, local copies, waits for them, and re-layouts: 2.62 us -> 10.9 us
    all_gather x1, waiting for transfers between devices: 62.9 us -> 55.6 us  [local(): key_piece = lax.all_gather(own_keys, 'ctx', axis=0, tiled=True)]
    ppermute x4, waiting for transfers between devices: 7.79 us -> 0.79 us  [swapped(): lax.ppermute(value, axis, [(i, i ^ 1 << stride) for i in range(lax.axis_s...]
    unnamed x1, blocking collectives: 28.6 us -> 34.2 us
  transfers between devices with their start and end apart: 7 -> 21, of which waited for: 7 -> 14; matrix products, arithmetic and copies ran while one was open for 3% -> 11% of each run, Pallas kernels for 0% -> 0%
where the time goes in v1:
time: 388 us; the launch traced here: 385 us
  waiting for transfers between devices  134 us (35%)
  matrix products  58.6 us (15%)
  starting transfers between devices  55.1 us (14%)
  other arithmetic  48.5 us (12%)
  local copies, waits for them, and re-layouts  34.9 us (9%)
  blocking collectives  34.2 us (9%)
  between operations  18.7 us (5%)
    ppermute x15, waiting for transfers between devices, set_balance(): lax.ppermute(kept_rows[-1], axis_name=peer_axis, perm=[(dev, (dev + 1) %...  77.7 us
    all_gather x1, waiting for transfers between devices, local(): key_piece = lax.all_gather(own_keys, 'ctx', axis=0, tiled=True)  55.6 us
    unnamed x1, blocking collectives  34.2 us
    ppermute x15, starting transfers between devices, set_balance(): lax.ppermute(kept_rows[-1], axis_name=peer_axis, perm=[(dev, (dev + 1) %...  28.7 us
    dot_general x16, matrix products, attend(): jnp.einsum('hij,jd->hid', exp_terms.astype(jnp.bfloat16), value_piece, pr...  27.7 us
    ppermute x4, starting transfers between devices, swapped(): lax.ppermute(value, axis, [(i, i ^ 1 << stride) for i in range(lax.axis_s...  26.4 us
    dot_general x16, matrix products, attend(): jnp.einsum('ihd,jd->hij', soft_rows, key_piece, preferred_element_type=jn...  23.3 us
    unnamed x59, local copies, waits for them, and re-layouts  10.9 us
  transfers between devices with their start and end apart: 21, of which 14 were waited for; matrix products, arithmetic and copies ran while one was open for 11% of the time, Pallas kernels for 0%

profile of v1, /device:TPU:1, one launch (start us, length us, event | category | flops | bytes accessed | tf_op | source)
XLA Modules:
  0.0 385.2 jit_solution(15965211139263131461)
XLA Ops:
  7.2 8.8 %collective-permute-start.2 = (bf16[512,32]{0,1:T(8,128)(2,1)}, bf16[512,32]{0,1:T(8,128)(2,1)S(1)}, u32[]{:S(2)}, u32[]{:S(2)}) collective-permute-start(bf16[512,32]{0,1:T(8,128)(2,1)} %param.21), channel_id=1, source_target_pairs={{0,1},{1,0},{2,3},{3,2},{4,5},{5,4},{6,7},{7,6},{8,9},{9,8},{10,11... | collective-permute-start | bytes 98312 | tf_op jit(solution)/shard_map/ppermute | solution.py:51
  26.9 1.9 collective-permute-start.3
  32.6 1.9 collective-permute-start.4
  35.1 6.9 %collective-permute-done.4 = bf16[512,128]{0,1:T(8,128)(2,1)S(1)} collective-permute-done((bf16[512,128]{0,1:T(8,128)(2,1)S(1)}, bf16[512,128]{0,1:T(8,128)(2,1)S(1)}, u32[]{:S(2)}, u32[]{:S(2)}) %collective-permute-start.4) | collective-permute-done | bytes 131104 | tf_op jit(solution)/shard_map/ppermute | solution.py:17
  42.0 1.9 collective-permute-start.5
  44.1 6.9 %collective-permute-done.5 = bf16[512,128]{0,1:T(8,128)(2,1)S(1)} collective-permute-done((bf16[512,128]{0,1:T(8,128)(2,1)S(1)}, bf16[512,128]{0,1:T(8,128)(2,1)S(1)}, u32[]{:S(2)}, u32[]{:S(2)}) %collective-permute-start.5) | collective-permute-done | bytes 131104 | tf_op jit(solution)/shard_map/ppermute | solution.py:17
  51.0 1.9 collective-permute-start.6
  53.5 6.5 %collective-permute-done.6 = bf16[512,128]{0,1:T(8,128)(2,1)S(1)} collective-permute-done((bf16[512,128]{0,1:T(8,128)(2,1)S(1)}, bf16[512,128]{0,1:T(8,128)(2,1)S(1)}, u32[]{:S(2)}, u32[]{:S(2)}) %collective-permute-start.6) | collective-permute-done | bytes 131104 | tf_op jit(solution)/shard_map/ppermute | solution.py:17
  60.0 1.9 collective-permute-start.7
  62.9 6.2 %collective-permute-done.7 = bf16[512,128]{0,1:T(8,128)(2,1)S(1)} collective-permute-done((bf16[512,128]{0,1:T(8,128)(2,1)S(1)}, bf16[512,128]{0,1:T(8,128)(2,1)S(1)}, u32[]{:S(2)}, u32[]{:S(2)}) %collective-permute-start.7) | collective-permute-done | bytes 131104 | tf_op jit(solution)/shard_map/ppermute | solution.py:17
  69.1 1.9 collective-permute-start.8
  71.0 7.1 %collective-permute-done.8 = bf16[512,128]{0,1:T(8,128)(2,1)S(1)} collective-permute-done((bf16[512,128]{0,1:T(8,128)(2,1)S(1)}, bf16[512,128]{0,1:T(8,128)(2,1)S(1)}, u32[]{:S(2)}, u32[]{:S(2)}) %collective-permute-start.8) | collective-permute-done | bytes 131104 | tf_op jit(solution)/shard_map/ppermute | solution.py:17
  78.1 1.9 collective-permute-start.9
  80.0 7.2 %collective-permute-done.9 = bf16[512,128]{0,1:T(8,128)(2,1)S(1)} collective-permute-done((bf16[512,128]{0,1:T(8,128)(2,1)S(1)}, bf16[512,128]{0,1:T(8,128)(2,1)S(1)}, u32[]{:S(2)}, u32[]{:S(2)}) %collective-permute-start.9) | collective-permute-done | bytes 131104 | tf_op jit(solution)/shard_map/ppermute | solution.py:17
  87.2 1.9 collective-permute-start.10
  89.1 7.1 %collective-permute-done.10 = bf16[512,128]{0,1:T(8,128)(2,1)S(1)} collective-permute-done((bf16[512,128]{0,1:T(8,128)(2,1)S(1)}, bf16[512,128]{0,1:T(8,128)(2,1)S(1)}, u32[]{:S(2)}, u32[]{:S(2)}) %collective-permute-start.10) | collective-permute-done | bytes 131104 | tf_op jit(solution)/shard_map/ppermute | solution.py:17
  96.2 1.9 collective-permute-start.11
  98.1 7.4 %collective-permute-done.11 = bf16[512,128]{0,1:T(8,128)(2,1)S(1)} collective-permute-done((bf16[512,128]{0,1:T(8,128)(2,1)S(1)}, bf16[512,128]{0,1:T(8,128)(2,1)S(1)}, u32[]{:S(2)}, u32[]{:S(2)}) %collective-permute-start.11) | collective-permute-done | bytes 131104 | tf_op jit(solution)/shard_map/ppermute | solution.py:17
  105.6 1.9 collective-permute-start.12
  107.5 13.3 %collective-permute-start = (bf16[512,32]{0,1:T(8,128)(2,1)}, bf16[512,32]{0,1:T(8,128)(2,1)S(1)}, u32[]{:S(2)}, u32[]{:S(2)}) collective-permute-start(bf16[512,32]{0,1:T(8,128)(2,1)} %param.20), channel_id=1, source_target_pairs={{0,1},{1,0},{2,3},{3,2},{4,5},{5,4},{6,7},{7,6},{8,9},{9,8},{10,11... | collective-permute-start | bytes 98312 | tf_op jit(solution)/shard_map/ppermute | solution.py:51
  120.8 1.9 collective-permute-start.13
  122.8 1.7 fusion.64
  124.5 5.7 %collective-permute-done.13 = bf16[512,128]{0,1:T(8,128)(2,1)S(1)} collective-permute-done((bf16[512,128]{0,1:T(8,128)(2,1)S(1)}, bf16[512,128]{0,1:T(8,128)(2,1)S(1)}, u32[]{:S(2)}, u32[]{:S(2)}) %collective-permute-start.13) | collective-permute-done | bytes 131104 | tf_op jit(solution)/shard_map/ppermute | solution.py:17
  130.2 1.9 collective-permute-start.14
  132.1 7.1 %collective-permute-done.14 = bf16[512,128]{0,1:T(8,128)(2,1)S(1)} collective-permute-done((bf16[512,128]{0,1:T(8,128)(2,1)S(1)}, bf16[512,128]{0,1:T(8,128)(2,1)S(1)}, u32[]{:S(2)}, u32[]{:S(2)}) %collective-permute-start.14) | collective-permute-done | bytes 131104 | tf_op jit(solution)/shard_map/ppermute | solution.py:17
  139.2 1.9 collective-permute-start.15
  141.9 6.3 %collective-permute-done.15 = bf16[512,128]{0,1:T(8,128)(2,1)S(1)} collective-permute-done((bf16[512,128]{0,1:T(8,128)(2,1)S(1)}, bf16[512,128]{0,1:T(8,128)(2,1)S(1)}, u32[]{:S(2)}, u32[]{:S(2)}) %collective-permute-start.15) | collective-permute-done | bytes 131104 | tf_op jit(solution)/shard_map/ppermute | solution.py:17
  148.2 1.9 collective-permute-start.16
  152.9 2.3 collective-permute-start.1
  155.3 3.2 collective-permute-done.16
  158.4 1.9 collective-permute-start.17
  160.9 34.2 %all-reduce = bf16[32]{0:T(256)(128)(2,1)} all-reduce(bf16[32]{0:T(256)(128)(2,1)S(1)} %dynamic-update-slice), channel_id=2, replica_groups=mesh['ctx'=16,'head'=32] {'ctx'}, use_global_device_ids=true, to_apply=%add | all-reduce | flops 32 | bytes 128
  199.1 1.7 copy.144
  200.8 1.6 maximum_select_fusion
  202.5 1.9 collective-permute-start.18
  204.5 1.6 fusion.32
  206.1 1.5 fusion.29
  207.6 1.9 fusion.31
  209.5 1.5 fusion.30
  212.1 1.5 fusion.35
  218.9 2.4 copy.124
  221.3 55.6 %all-gather.5.cloned.1.call-done = bf16[8192,128]{0,1:T(8,128)(2,1)} async-done(((bf16[512,128]{0,1:T(8,128)(2,1)}), bf16[8192,128]{0,1:T(8,128)(2,1)}) %all-gather.5.cloned.1.call-update) | async-done | bytes 2097168 | tf_op jit(solution)/shard_map/all_gather | solution.py:190
  276.9 4.1 %copy.122 = bf16[8192,128]{1,0:T(8,128)(2,1)} copy(bf16[8192,128]{0,1:T(8,128)(2,1)} %all-gather.5.cloned.1.call-done) | data formatting | bytes 4194304 | tf_op jit(solution)/shard_map/all_gather | solution.py:190
  281.0 96.5 %while.30 = (s32[]{:T(128)}, f32[2,512]{1,0:T(2,128)S(1)}, f32[2,512]{1,0:T(2,128)S(1)}, f32[2,512,128]{2,1,0:T(8,128)S(1)}, s32[16]{0:T(128)S(1)}, /*index=5*/s...) while((s32[]{:T(128)}, f32[2,512]{1,0:T(2,128)S(1)}, ...), condition=%wide.region_15.16_spmd.clone, body=%wide.region_11.15_spmd.clone.sunk | while | flops 275395584 | bytes 9000113 | solution.py:199
  283.3 1.5 fusion.92
  285.3 1.7 convolution_add_fusion.3
  289.3 1.5 fusion.92
  291.3 1.7 convolution_add_fusion.3
  297.3 1.7 convolution_add_fusion.3
  303.4 1.7 convolution_add_fusion.3
  307.4 1.5 fusion.92
  309.4 1.7 convolution_add_fusion.3
  315.4 1.7 convolution_add_fusion.3
  321.5 1.7 convolution_add_fusion.3
  325.5 1.5 fusion.92
  327.5 1.7 convolution_add_fusion.3
  333.5 1.7 convolution_add_fusion.3
  339.5 1.7 convolution_add_fusion.3
  345.6 1.7 convolution_add_fusion.3
  351.6 1.7 convolution_add_fusion.3
  357.6 1.7 convolution_add_fusion.3
  363.7 1.7 convolution_add_fusion.3
  369.7 1.7 convolution_add_fusion.3
  375.7 1.7 convolution_add_fusion.3
  (277 shorter events, 89.8 us)
Async XLA Ops:
  7.2 145.1 %copy-start.3 = (bf16[512,32]{0,1:T(8,128)(2,1)S(1)}, bf16[512,32]{0,1:T(8,128)(2,1)}, u32[]{:S(2)}) copy-start(bf16[512,32]{0,1:T(8,128)(2,1)} %param.20) | copy-start | bytes 98308
  7.2 197.2 %all-gather.7.cloned.1.call-start = ((), (), s32[]{:S(2)}) async-start(), calls=%async_computation.1 | async-start | bytes 1114112 | tf_op jit(solution)/shard_map/all_gather | solution.py:33
  7.2 18.9 %collective-permute-start.2 = (bf16[512,32]{0,1:T(8,128)(2,1)}, bf16[512,32]{0,1:T(8,128)(2,1)S(1)}, u32[]{:S(2)}, u32[]{:S(2)}) collective-permute-start(bf16[512,32]{0,1:T(8,128)(2,1)} %param.21), channel_id=1, source_target_pairs={{0,1},{1,0},{2,3},{3,2},{4,5},{5,4},{6,7},{7,6},{8,9},{9,8},{10,11... | collective-permute-start | bytes 98312 | tf_op jit(solution)/shard_map/ppermute | solution.py:51
  26.9 5.6 %collective-permute-start.3 = (bf16[512,64]{0,1:T(8,128)(2,1)S(1)}, bf16[512,64]{0,1:T(8,128)(2,1)S(1)}, u32[]{:S(2)}, u32[]{:S(2)}) collective-permute-start(bf16[512,64]{0,1:T(8,128)(2,1)S(1)} %maximum_select_fusion.3), channel_id=1, source_target_pairs={{0,2},{1,3},{2,0},{3,1},{4,6},{5,7},{6,4},{7,5},{8,10},{9,11},{10,... | collective-permute-start | bytes 196616 | tf_op jit(solution)/shard_map/ppermute | solution.py:51
  31.0 0.8 copy-start.4
  31.1 3.4 copy-start.5
  32.6 9.4 %collective-permute-start.4 = (bf16[512,128]{0,1:T(8,128)(2,1)S(1)}, bf16[512,128]{0,1:T(8,128)(2,1)S(1)}, u32[]{:S(2)}, u32[]{:S(2)}) collective-permute-start(bf16[512,128]{0,1:T(8,128)(2,1)S(1)} %maximum_select_fusion.1), channel_id=1, source_target_pairs={{0,32},{32,64},{64,96},{96,128},{128,160},{160,192},{192,224},{224... | collective-permute-start | bytes 393224 | tf_op jit(solution)/shard_map/ppermute | solution.py:17
  42.0 9.0 %collective-permute-start.5 = (bf16[512,128]{0,1:T(8,128)(2,1)S(1)}, bf16[512,128]{0,1:T(8,128)(2,1)S(1)}, u32[]{:S(2)}, u32[]{:S(2)}) collective-permute-start(bf16[512,128]{0,1:T(8,128)(2,1)S(1)} %collective-permute-done.4), channel_id=1, source_target_pairs={{0,32},{32,64},{64,96},{96,128},{128,160},{160,192},{192,224},{224... | collective-permute-start | bytes 393224 | tf_op jit(solution)/shard_map/ppermute | solution.py:17
  51.0 9.0 %collective-permute-start.6 = (bf16[512,128]{0,1:T(8,128)(2,1)S(1)}, bf16[512,128]{0,1:T(8,128)(2,1)S(1)}, u32[]{:S(2)}, u32[]{:S(2)}) collective-permute-start(bf16[512,128]{0,1:T(8,128)(2,1)S(1)} %collective-permute-done.5), channel_id=1, source_target_pairs={{0,32},{32,64},{64,96},{96,128},{128,160},{160,192},{192,224},{224... | collective-permute-start | bytes 393224 | tf_op jit(solution)/shard_map/ppermute | solution.py:17
  60.0 9.0 %collective-permute-start.7 = (bf16[512,128]{0,1:T(8,128)(2,1)S(1)}, bf16[512,128]{0,1:T(8,128)(2,1)S(1)}, u32[]{:S(2)}, u32[]{:S(2)}) collective-permute-start(bf16[512,128]{0,1:T(8,128)(2,1)S(1)} %collective-permute-done.6), channel_id=1, source_target_pairs={{0,32},{32,64},{64,96},{96,128},{128,160},{160,192},{192,224},{224... | collective-permute-start | bytes 393224 | tf_op jit(solution)/shard_map/ppermute | solution.py:17
  62.8 214.1 %all-gather.5.cloned.1.call-start = ((), (), s32[]{:S(2)}) async-start(), calls=%async_computation | async-start | bytes 2228224 | tf_op jit(solution)/shard_map/all_gather | solution.py:190
  69.1 9.0 %collective-permute-start.8 = (bf16[512,128]{0,1:T(8,128)(2,1)S(1)}, bf16[512,128]{0,1:T(8,128)(2,1)S(1)}, u32[]{:S(2)}, u32[]{:S(2)}) collective-permute-start(bf16[512,128]{0,1:T(8,128)(2,1)S(1)} %collective-permute-done.7), channel_id=1, source_target_pairs={{0,32},{32,64},{64,96},{96,128},{128,160},{160,192},{192,224},{224... | collective-permute-start | bytes 393224 | tf_op jit(solution)/shard_map/ppermute | solution.py:17
  78.1 9.1 %collective-permute-start.9 = (bf16[512,128]{0,1:T(8,128)(2,1)S(1)}, bf16[512,128]{0,1:T(8,128)(2,1)S(1)}, u32[]{:S(2)}, u32[]{:S(2)}) collective-permute-start(bf16[512,128]{0,1:T(8,128)(2,1)S(1)} %collective-permute-done.8), channel_id=1, source_target_pairs={{0,32},{32,64},{64,96},{96,128},{128,160},{160,192},{192,224},{224... | collective-permute-start | bytes 393224 | tf_op jit(solution)/shard_map/ppermute | solution.py:17
  87.2 9.1 %collective-permute-start.10 = (bf16[512,128]{0,1:T(8,128)(2,1)S(1)}, bf16[512,128]{0,1:T(8,128)(2,1)S(1)}, u32[]{:S(2)}, u32[]{:S(2)}) collective-permute-start(bf16[512,128]{0,1:T(8,128)(2,1)S(1)} %collective-permute-done.9), channel_id=1, source_target_pairs={{0,32},{32,64},{64,96},{96,128},{128,160},{160,192},{192,224},{224... | collective-permute-start | bytes 393224 | tf_op jit(solution)/shard_map/ppermute | solution.py:17
  96.2 9.4 %collective-permute-start.11 = (bf16[512,128]{0,1:T(8,128)(2,1)S(1)}, bf16[512,128]{0,1:T(8,128)(2,1)S(1)}, u32[]{:S(2)}, u32[]{:S(2)}) collective-permute-start(bf16[512,128]{0,1:T(8,128)(2,1)S(1)} %collective-permute-done.10), channel_id=1, source_target_pairs={{0,32},{32,64},{64,96},{96,128},{128,160},{160,192},{192,224},{224... | collective-permute-start | bytes 393224 | tf_op jit(solution)/shard_map/ppermute | solution.py:17
  105.6 15.3 %collective-permute-start.12 = (bf16[512,128]{0,1:T(8,128)(2,1)S(1)}, bf16[512,128]{0,1:T(8,128)(2,1)S(1)}, u32[]{:S(2)}, u32[]{:S(2)}) collective-permute-start(bf16[512,128]{0,1:T(8,128)(2,1)S(1)} %collective-permute-done.11), channel_id=1, source_target_pairs={{0,32},{32,64},{64,96},{96,128},{128,160},{160,192},{192,224},{224... | collective-permute-start | bytes 393224 | tf_op jit(solution)/shard_map/ppermute | solution.py:17
  107.5 44.8 %collective-permute-start = (bf16[512,32]{0,1:T(8,128)(2,1)}, bf16[512,32]{0,1:T(8,128)(2,1)S(1)}, u32[]{:S(2)}, u32[]{:S(2)}) collective-permute-start(bf16[512,32]{0,1:T(8,128)(2,1)} %param.20), channel_id=1, source_target_pairs={{0,1},{1,0},{2,3},{3,2},{4,5},{5,4},{6,7},{7,6},{8,9},{9,8},{10,11... | collective-permute-start | bytes 98312 | tf_op jit(solution)/shard_map/ppermute | solution.py:51
  120.8 9.3 %collective-permute-start.13 = (bf16[512,128]{0,1:T(8,128)(2,1)S(1)}, bf16[512,128]{0,1:T(8,128)(2,1)S(1)}, u32[]{:S(2)}, u32[]{:S(2)}) collective-permute-start(bf16[512,128]{0,1:T(8,128)(2,1)S(1)} %collective-permute-done.12), channel_id=1, source_target_pairs={{0,32},{32,64},{64,96},{96,128},{128,160},{160,192},{192,224},{224... | collective-permute-start | bytes 393224 | tf_op jit(solution)/shard_map/ppermute | solution.py:17
  130.2 9.0 %collective-permute-start.14 = (bf16[512,128]{0,1:T(8,128)(2,1)S(1)}, bf16[512,128]{0,1:T(8,128)(2,1)S(1)}, u32[]{:S(2)}, u32[]{:S(2)}) collective-permute-start(bf16[512,128]{0,1:T(8,128)(2,1)S(1)} %collective-permute-done.13), channel_id=1, source_target_pairs={{0,32},{32,64},{64,96},{96,128},{128,160},{160,192},{192,224},{224... | collective-permute-start | bytes 393224 | tf_op jit(solution)/shard_map/ppermute | solution.py:17
  139.2 9.0 %collective-permute-start.15 = (bf16[512,128]{0,1:T(8,128)(2,1)S(1)}, bf16[512,128]{0,1:T(8,128)(2,1)S(1)}, u32[]{:S(2)}, u32[]{:S(2)}) collective-permute-start(bf16[512,128]{0,1:T(8,128)(2,1)S(1)} %collective-permute-done.14), channel_id=1, source_target_pairs={{0,32},{32,64},{64,96},{96,128},{128,160},{160,192},{192,224},{224... | collective-permute-start | bytes 393224 | tf_op jit(solution)/shard_map/ppermute | solution.py:17
  148.2 10.2 %collective-permute-start.16 = (bf16[512,128]{0,1:T(8,128)(2,1)S(1)}, bf16[512,128]{0,1:T(8,128)(2,1)S(1)}, u32[]{:S(2)}, u32[]{:S(2)}) collective-permute-start(bf16[512,128]{0,1:T(8,128)(2,1)S(1)} %collective-permute-done.15), channel_id=1, source_target_pairs={{0,32},{32,64},{64,96},{96,128},{128,160},{160,192},{192,224},{224... | collective-permute-start | bytes 393224 | tf_op jit(solution)/shard_map/ppermute | solution.py:17
  152.9 47.9 %collective-permute-start.1 = (bf16[512,64]{0,1:T(8,128)(2,1)}, bf16[512,64]{0,1:T(8,128)(2,1)}, u32[]{:S(2)}, u32[]{:S(2)}) collective-permute-start(bf16[512,64]{0,1:T(8,128)(2,1)} %maximum_select_fusion.2), channel_id=1, source_target_pairs={{0,2},{1,3},{2,0},{3,1},{4,6},{5,7},{6,4},{7,5},{8,10},{9,11},{10,... | collective-permute-start | bytes 196616 | tf_op jit(solution)/shard_map/ppermute | solution.py:51
  158.4 46.0 %copy-start = (bf16[512,128]{0,1:T(8,128)(2,1)}, bf16[512,128]{0,1:T(8,128)(2,1)S(1)}, u32[]{:S(2)}) copy-start(bf16[512,128]{0,1:T(8,128)(2,1)S(1)} %collective-permute-done.16) | copy-start | bytes 393220
  158.4 44.0 %collective-permute-start.17 = (bf16[512,128]{0,1:T(8,128)(2,1)S(1)}, bf16[512,128]{0,1:T(8,128)(2,1)}, u32[]{:S(2)}, u32[]{:S(2)}) collective-permute-start(bf16[512,128]{0,1:T(8,128)(2,1)S(1)} %collective-permute-done.16), channel_id=1, source_target_pairs={{0,32},{32,64},{64,96},{96,128},{128,160},{160,192},{192,224},{224... | collective-permute-start | bytes 393224 | tf_op jit(solution)/shard_map/ppermute | solution.py:17
  199.1 7.0 %copy-start.2 = (bf16[256,256]{0,1:T(8,128)(2,1)}, bf16[256,256]{0,1:T(8,128)(2,1)S(1)}, u32[]{:S(2)}) copy-start(bf16[256,256]{0,1:T(8,128)(2,1)S(1)} %copy.138) | copy-start | bytes 393220
  202.5 11.1 %collective-permute-start.18 = (bf16[512,128]{0,1:T(8,128)(2,1)}, bf16[512,128]{0,1:T(8,128)(2,1)}, u32[]{:S(2)}, u32[]{:S(2)}) collective-permute-start(bf16[512,128]{0,1:T(8,128)(2,1)} %collective-permute-done.17), channel_id=1, source_target_pairs={{0,32},{32,64},{64,96},{96,128},{128,160},{160,192},{192,224},{224... | collective-permute-start | bytes 393224 | tf_op jit(solution)/shard_map/ppermute | solution.py:17
  211.5 6.9 %copy-start.1 = (bf16[512,128]{0,1:T(8,128)(2,1)S(1)}, bf16[512,128]{0,1:T(8,128)(2,1)}, u32[]{:S(2)}) copy-start(bf16[512,128]{0,1:T(8,128)(2,1)} %copy-done) | copy-start | bytes 393220
  218.9 62.2 %copy-start.6 = (s32[16]{0:T(128)S(1)}, s32[16]{0:T(128)}, u32[]{:S(2)}) copy-start(s32[16]{0:T(128)} %iota_multiply_fusion) | copy-start | bytes 196
Sparse Core Ops, SparseCore 0:
  62.9 61.5 all-gather.6
  202.6 74.3 all-gather.4
